TPU v7x, 256 devices: a whole 4x4x8 slice. The times are simulated.
256 devices in a mesh: seq: 64 (over z, y, core), tensor: 4 (over x).
Axes of the slice: x: 4, y: 4, z: 8, core: 2. Of those that a mesh axis runs over, the one named last changes fastest.
Arguments:
- tokens: bfloat16 [32768, 2048], P('seq', 'tensor')
- norm_gain: float32 [2048], replicated, may hold values from 0.5 to 1.5
- w_qkv: bfloat16 [2048, 4, 1024], P(None, 'tensor'), may hold values from -0.125 to 0.125
- w_gate_out: bfloat16 [2048, 2048], P(None, 'tensor'), may hold values from -0.125 to 0.125
- gate_down: bfloat16 [2048, 16], replicated
- gate_up: float32 [16, 4, 256], P(None, 'tensor')
- gate_bias: float32 [4, 256], P('tensor')
- conv_weight: float32 [4, 4, 1024], P(None, 'tensor'), may hold values from -3 to 3
- head_gain: float32 [512], replicated, may hold values from 0.5 to 1.5
- w_out: bfloat16 [2048, 2048], P('tensor'), may hold values from -0.125 to 0.125
- spans: int32 [3], replicated, may hold values from 1 to 48, 64 in all
- fills: int32 [3], replicated, may hold values from 1 to 512
- request_prompt: int32 [128], P('seq'), may hold values from -1 to 2, as said below
Outputs:
- mixed: bfloat16 [32768, 2048], P(('seq', 'tensor'))
- owner_state: float32 [128, 4, 256, 512], P('seq', 'tensor')
- owner_edge: bfloat16 [128, 3, 4, 1024], P('seq', None, 'tensor')
Inputs may be any that keep to these rules, and one draw needn't show every extreme that they name: `spans`: the prompts lie along seq in order and together cover all its indices. `request_prompt`: slots r * 2 to r * 2 + 1 belong to index r of seq; the first slot of every index names a prompt; every prompt is named by some slot.
All inputs are finite; a program needn't handle non-finite values.
Results may differ from a plain program's by a relative error of at most 0.0095.
Values may be sent and summed in bfloat16 or wider, within the bound.
A program may use at most 128 MiB of HBM per device.

v0:
```python
import jax
import jax.numpy as jnp
from jax import lax
from jax.sharding import PartitionSpec as P

STRETCH = 64
EPS_IN = 1e-06
EPS_HEAD = 1e-05
EXACT_MATMUL = lax.Precision.HIGHEST


def from_behind(array, axis, by):
    peers = lax.axis_size(axis)
    pairs = [(i, i + by) for i in range(peers) if 0 <= i + by < peers]
    return lax.ppermute(array, axis, pairs)


def broadcast(block, axis, source):
    block = jnp.where(lax.axis_index(axis) == source, block, jnp.zeros_like(block))
    return lax.psum(block, axis)


def block_pass(carry, pieces):
    passed_along_state, offset = carry
    q_blk, k_blk, value_block, decay_blk = pieces
    block_rows = q_blk.shape[0]
    k_wide = k_blk.astype(jnp.float32)
    cumulative = jnp.cumsum(decay_blk, axis=0)
    query_decayed = (q_blk * jnp.exp(cumulative)).astype(jnp.bfloat16)
    pair_decay = jnp.exp(jnp.minimum(cumulative[:, None] - cumulative[None, :], 0.0))
    causal_mask = jnp.arange(block_rows)[:, None] >= jnp.arange(block_rows)[None, :]
    scores = jnp.einsum("ihk,jhk,ijhk->hij", q_blk, k_wide, pair_decay, precision=EXACT_MATMUL)
    scores = jnp.where(causal_mask[None], scores, 0.0).astype(jnp.bfloat16)
    intra_term = jnp.einsum("hij,jhv->ihv", scores, value_block, preferred_element_type=jnp.float32)
    closing_decay = cumulative[-1]
    weight_applied = (k_wide * jnp.exp(closing_decay[None] - cumulative)).astype(jnp.bfloat16)
    updated = jnp.exp(closing_decay)[:, :, None] * passed_along_state + jnp.einsum(
        "qbr,qbp->brp", weight_applied, value_block, preferred_element_type=jnp.float32
    )
    return (
        (updated, offset + closing_decay),
        (intra_term, passed_along_state, offset, query_decayed),
    )


def body(
    tokens,
    norm_gain,
    w_qkv,
    w_gate_out,
    gate_down,
    gate_up,
    gate_bias,
    conv_weight,
    head_gain,
    w_out,
    spans,
    fills,
    request_prompt,
):
    row_count = tokens.shape[0]
    local_heads = w_qkv.shape[1]
    width_qkv = w_qkv.shape[2]
    key_width = gate_up.shape[2]
    value_width = head_gain.shape[0]
    model_width = norm_gain.shape[0]
    taps = conv_weight.shape[0]
    prompts = spans.shape[0]
    slot_count = request_prompt.shape[0]
    seq_index = lax.axis_index("seq")
    span_ends = jnp.cumsum(spans)
    starts = span_ends - spans
    my_prompt = jnp.sum((span_ends <= seq_index).astype(jnp.int32))
    picked = jnp.arange(prompts, dtype=jnp.int32) == my_prompt
    first_dev = jnp.sum(jnp.where(picked, starts, 0))
    last_dev = jnp.sum(jnp.where(picked, span_ends - 1, 0))
    is_start = seq_index == first_dev
    is_last = seq_index == last_dev
    live_rows = jnp.where(is_last, jnp.sum(jnp.where(picked, fills, 0)), row_count)
    valid = jnp.arange(row_count, dtype=jnp.int32) < live_rows
    value_entries = tokens.astype(jnp.float32)
    squares = lax.psum(jnp.sum(value_entries * value_entries, axis=1), "tensor")
    inverse = lax.rsqrt(squares / model_width + EPS_IN)
    flat_qkv = w_qkv.reshape(model_width, local_heads * width_qkv)
    normed = (
        lax.all_gather(tokens, "tensor", axis=1, tiled=True).astype(jnp.float32)
        * inverse[:, None]
        * norm_gain[None, :]
    ).astype(jnp.bfloat16)
    qkv_sum = jnp.dot(normed, flat_qkv, preferred_element_type=jnp.float32)
    gate_sum = jnp.dot(normed, w_gate_out, preferred_element_type=jnp.float32)
    low_rank = jnp.dot(normed, gate_down, preferred_element_type=jnp.float32)
    projected = qkv_sum.astype(jnp.bfloat16).reshape(row_count, local_heads, width_qkv)
    gate_rounded = lax.optimization_barrier(gate_sum.astype(jnp.bfloat16))
    gate_values = gate_rounded.astype(jnp.float32).reshape(row_count, local_heads, value_width)
    logits = jnp.dot(
        low_rank, gate_up.reshape(gate_up.shape[0], local_heads * key_width), precision=EXACT_MATMUL
    )
    logits = logits.reshape(row_count, local_heads, key_width) + gate_bias[None]
    log_decay = jnp.where(valid[:, None, None], jax.nn.log_sigmoid(logits) / 16.0, 0.0)
    tail_rows = projected[row_count - taps + 1 :]
    previous = from_behind(tail_rows, "seq", 1)
    previous = jnp.where(is_start, jnp.zeros_like(previous), previous)
    extended = jnp.concatenate([previous, projected], axis=0)
    conv_sum = jnp.zeros((row_count, local_heads, width_qkv), jnp.float32)
    for offset in range(taps):
        conv_sum = conv_sum + conv_weight[offset][None] * extended[
            offset : offset + row_count
        ].astype(jnp.float32)
    activated = jax.nn.silu(conv_sum).astype(jnp.bfloat16)
    query_rows = activated[:, :, :key_width].astype(jnp.float32) * key_width ** (-0.5)
    key_rows = jnp.where(
        valid[:, None, None],
        activated[:, :, key_width : 2 * key_width],
        jnp.zeros((), jnp.bfloat16),
    )
    value_rows = activated[:, :, 2 * key_width :]

    def into_blocks(array):
        return array.reshape(row_count // STRETCH, STRETCH, local_heads, array.shape[-1])

    start_carry = (
        jnp.zeros((local_heads, key_width, value_width), jnp.float32),
        jnp.zeros((local_heads, key_width), jnp.float32),
    )
    (local_state, decay_sum), (local_out, block_starts, block_offsets, query_decayed) = lax.scan(
        block_pass,
        start_carry,
        (
            into_blocks(query_rows),
            into_blocks(key_rows),
            into_blocks(value_rows),
            into_blocks(log_decay),
        ),
    )
    decay_total = jnp.exp(decay_sum)
    span_most = 3 * lax.axis_size("seq") // 4

    def relay(turn, carry):
        received, outgoing = carry
        received = from_behind(outgoing, "seq", 1)
        received = jnp.where(is_start, jnp.zeros_like(received), received)
        return (received, decay_total[:, :, None] * received + local_state)

    incoming, _ = lax.fori_loop(0, span_most - 1, relay, (jnp.zeros_like(local_state), local_state))
    full_starts = block_starts + jnp.exp(block_offsets)[:, :, :, None] * incoming[None]
    cross_block_term = jnp.einsum(
        "bchk,bhkv->bchv",
        query_decayed,
        full_starts.astype(jnp.bfloat16),
        preferred_element_type=jnp.float32,
    )
    attended = (cross_block_term + local_out).reshape(row_count, local_heads, value_width)
    end_state = decay_total[:, :, None] * incoming + local_state
    mean_square = jnp.mean(attended * attended, axis=2, keepdims=True)
    gated = (
        attended
        * lax.rsqrt(mean_square + EPS_HEAD)
        * head_gain[None, None, :]
        * jax.nn.silu(gate_values)
    ).astype(jnp.bfloat16)
    gated = gated.reshape(row_count, local_heads * value_width)
    share = row_count // lax.axis_size("tensor")
    summed = lax.psum_scatter(
        jnp.dot(gated, w_out, preferred_element_type=jnp.float32).astype(jnp.bfloat16),
        "tensor",
        scatter_dimension=0,
        tiled=True,
    ).astype(jnp.float32)
    own_rows = lax.axis_index("tensor") * share + jnp.arange(share, dtype=jnp.int32)
    mixed = jnp.where((own_rows < live_rows)[:, None], summed, 0.0).astype(jnp.bfloat16)
    edge_rows = lax.dynamic_slice_in_dim(extended, live_rows, taps - 1, 0)
    edge_wide = edge_rows.astype(jnp.float32)

    def deliver(turn, carry):
        states_sofar, edges_sofar = carry
        root = jnp.sum(jnp.where(jnp.arange(prompts, dtype=jnp.int32) == turn, span_ends - 1, 0))
        got_state, got_edge = (
            broadcast(end_state.astype(jnp.bfloat16), "seq", root).astype(end_state.dtype),
            broadcast(edge_wide.astype(jnp.bfloat16), "seq", root).astype(edge_wide.dtype),
        )
        wanted = (request_prompt == turn)[:, None, None, None]
        return (
            jnp.where(wanted, got_state[None], states_sofar),
            jnp.where(wanted, got_edge[None], edges_sofar),
        )

    empty = (
        jnp.zeros((slot_count, local_heads, key_width, value_width), jnp.float32),
        jnp.zeros((slot_count, taps - 1, local_heads, width_qkv), jnp.float32),
    )
    owner_state, owner_wide = lax.fori_loop(0, prompts, deliver, empty)
    owner_edge = owner_wide.astype(jnp.bfloat16)
    return (mixed, owner_state, owner_edge)


def solution(mesh):
    return jax.shard_map(
        body,
        mesh=mesh,
        in_specs=(
            P("seq", "tensor"),
            P(),
            P(None, "tensor", None),
            P(None, "tensor"),
            P(),
            P(None, "tensor", None),
            P("tensor", None),
            P(None, "tensor", None),
            P(),
            P("tensor", None),
            P(),
            P(),
            P("seq"),
        ),
        out_specs=(
            P(("seq", "tensor"), None),
            P("seq", "tensor", None, None),
            P("seq", None, "tensor", None),
        ),
        check_vma=False,
    )
```

profile of v0, /device:TPU:1, one launch (start us, length us, event | category | flops | bytes accessed | tf_op | source)
XLA Modules:
  0.0 1430.1 jit_solution(8142053873680387150)
XLA Ops:
  14.6 9.3 psum.35
  24.7 22.1 %all-gather.2.cloned.1.call-done = bf16[512,2048]{1,0:T(8,128)(2,1)} async-done(((bf16[512,512]{1,0:T(8,128)(2,1)}), bf16[512,2048]{1,0:T(8,128)(2,1)}) %all-gather.2.cloned.1.call-update) | async-done | bytes 2097168 | tf_op jit(solution)/shard_map/all_gather | solution.py:86
  64.2 61.5 %while.52 = (s32[]{:T(128)}, f32[1,256,512]{2,1,0:T(8,128)S(1)}, f32[1,256]{1,0:T(1,128)S(1)}, f32[8,64,1,512]{3,1,2,0:T(8,128)}, f32[8,1,256,512]{3,2,1,0:T(8,1...) while((s32[]{:T(128)}, f32[1,256,512]{2,1,0:T(8,128)S(1)}, ...), condition=%wide.region_9.10_spmd.clone, body=%wide.region_7.9_spmd.clone.sunk | while | flops 27890436 | bytes 12177578 | solution.py:126
  126.6 613.5 %while.51 = (s32[]{:T(128)}, f32[1,256,512]{2,1,0:T(8,128)}, f32[1,256,512]{2,1,0:T(8,128)}, pred[]{:T(512)}, f32[1,256]{1,0:T(1,128)S(1)}, /*index=5*/f32[1,256,512]{2,1,0:T(8,128)S(1)}, s32[]{:T(128)}) while((s32[]{:T(128)}, f32[1,256,512]{2,1,0:T(8,128)}, f32[1,256,512]{2,1,0:T(8,128)}, pred[]{:T(512)}, f32[1,256]{1,0:T(1,128)S(1)}, ...), condition=%wide.region_11.12_spmd, body=%wide.region_10.11_spmd.sunk | while | flops 393218 | bytes 4195446 | solution.py:145
  140.4 6.4 collective-permute-done
  152.2 6.4 collective-permute-done
  175.8 6.4 collective-permute-done
  199.4 6.4 collective-permute-done
  211.2 6.4 collective-permute-done
  223.0 6.4 collective-permute-done
  234.8 6.4 collective-permute-done
  258.5 6.4 collective-permute-done
  282.1 6.4 collective-permute-done
  293.9 6.4 collective-permute-done
  305.7 6.4 collective-permute-done
  317.5 6.4 collective-permute-done
  356.9 6.4 collective-permute-done
  370.8 6.4 collective-permute-done
  412.5 6.4 collective-permute-done
  426.4 6.4 collective-permute-done
  454.2 6.4 collective-permute-done
  468.2 6.4 collective-permute-done
  482.1 6.4 collective-permute-done
  509.9 6.4 collective-permute-done
  748.9 640.3 %while.53 = (s32[]{:T(128)}, f32[2,1,256,512]{3,2,1,0:T(8,128)S(1)}, bf16[2,3,1,1024]{3,2,1,0:T(2,128)(2,1)S(1)}, s32[2]{0:T(128)S(1)}, s32[3]{0:T(128)S(1)}, /*...) while((s32[]{:T(128)}, ...), condition=%wide.region_18.19_spmd.clone, body=%wide.region_14.18_spmd.clone.sunk | while | flops 935956 | bytes 5560569 | solution.py:192
  750.9 160.4 %psum.41 = bf16[3,1024]{1,0:T(4,128)(2,1)S(1)} all-reduce(bf16[3,1024]{1,0:T(4,128)(2,1)S(1)} %select_bitcast_fusion.5), channel_id=1, replica_groups=mesh['seq'=64,'tensor'=4] {'seq'}, use_global_device_ids=true, to_apply=%region_17.17 | all-reduce | flops 3072 | bytes 12288 | tf_op jit(solution)/shard_map/while/body/eval_jaxpr/psum | solution.py:20
  911.5 114.8 %all-reduce.2.cloned.1.call-done = bf16[256,512]{1,0:T(8,128)(2,1)} async-done(((bf16[256,512]{1,0:T(8,128)(2,1)}), bf16[256,512]{1,0:T(8,128)(2,1)}) %all-reduce.2.cloned.1.call-update) | async-done | bytes 262160 | tf_op jit(solution)/shard_map/while/body/eval_jaxpr/psum | solution.py:20
  1029.7 124.7 %psum.41 = bf16[3,1024]{1,0:T(4,128)(2,1)S(1)} all-reduce(bf16[3,1024]{1,0:T(4,128)(2,1)S(1)} %select_bitcast_fusion.5), channel_id=1, replica_groups=mesh['seq'=64,'tensor'=4] {'seq'}, use_global_device_ids=true, to_apply=%region_17.17 | all-reduce | flops 3072 | bytes 12288 | tf_op jit(solution)/shard_map/while/body/eval_jaxpr/psum | solution.py:20
  1154.5 52.8 %all-reduce.2.cloned.1.call-done = bf16[256,512]{1,0:T(8,128)(2,1)} async-done(((bf16[256,512]{1,0:T(8,128)(2,1)}), bf16[256,512]{1,0:T(8,128)(2,1)}) %all-reduce.2.cloned.1.call-update) | async-done | bytes 262160 | tf_op jit(solution)/shard_map/while/body/eval_jaxpr/psum | solution.py:20
  1210.7 124.6 %psum.41 = bf16[3,1024]{1,0:T(4,128)(2,1)S(1)} all-reduce(bf16[3,1024]{1,0:T(4,128)(2,1)S(1)} %select_bitcast_fusion.5), channel_id=1, replica_groups=mesh['seq'=64,'tensor'=4] {'seq'}, use_global_device_ids=true, to_apply=%region_17.17 | all-reduce | flops 3072 | bytes 12288 | tf_op jit(solution)/shard_map/while/body/eval_jaxpr/psum | solution.py:20
  1335.4 52.5 %all-reduce.2.cloned.1.call-done = bf16[256,512]{1,0:T(8,128)(2,1)} async-done(((bf16[256,512]{1,0:T(8,128)(2,1)}), bf16[256,512]{1,0:T(8,128)(2,1)}) %all-reduce.2.cloned.1.call-update) | async-done | bytes 262160 | tf_op jit(solution)/shard_map/while/body/eval_jaxpr/psum | solution.py:20
  1390.4 31.2 %reduce-scatter.2.cloned.1.call-done = bf16[128,2048]{1,0:T(8,128)(2,1)} async-done(((bf16[512,2048]{1,0:T(8,128)(2,1)}), bf16[128,2048]{1,0:T(8,128)(2,1)}) %reduce-scatter.2.cloned.1.call-update) | async-done | bytes 524304 | tf_op jit(solution)/shard_map/reduce_scatter | solution.py:164
  (370 shorter events, 590.3 us)
Async XLA Ops:
  7.2 39.6 %all-gather.2.cloned.1.call-start = ((), (), s32[]{:S(2)}) async-start(), calls=%async_computation.1 | async-start | bytes 2621440 | tf_op jit(solution)/shard_map/all_gather | solution.py:86
  350.5 12.8 collective-permute-start
  364.4 12.8 collective-permute-start
  378.3 12.8 collective-permute-start
  392.2 12.8 collective-permute-start
  406.1 12.8 collective-permute-start
  420.0 12.8 collective-permute-start
  433.9 12.8 collective-permute-start
  447.9 12.8 collective-permute-start
  461.8 12.8 collective-permute-start
  475.7 12.8 collective-permute-start
  489.6 12.8 collective-permute-start
  503.5 12.8 collective-permute-start
  517.4 12.8 collective-permute-start
  531.3 12.8 collective-permute-start
  545.2 12.8 collective-permute-start
  559.2 12.8 collective-permute-start
  573.1 12.8 collective-permute-start
  587.0 12.8 collective-permute-start
  600.9 12.8 collective-permute-start
  614.8 12.8 collective-permute-start
  628.7 12.8 collective-permute-start
  642.6 12.8 collective-permute-start
  656.5 12.8 collective-permute-start
  670.4 12.8 collective-permute-start
  684.4 12.8 collective-permute-start
  712.2 12.8 collective-permute-start
  726.1 12.8 collective-permute-start
  748.9 277.5 %all-reduce.2.cloned.1.call-start = ((), (), s32[]{:S(2)}) async-start(), calls=%async_computation.3 | async-start | bytes 524288 | tf_op jit(solution)/shard_map/while/body/eval_jaxpr/psum | solution.py:20
  1027.6 179.7 %all-reduce.2.cloned.1.call-start = ((), (), s32[]{:S(2)}) async-start(), calls=%async_computation.3 | async-start | bytes 524288 | tf_op jit(solution)/shard_map/while/body/eval_jaxpr/psum | solution.py:20
  1208.6 179.3 %all-reduce.2.cloned.1.call-start = ((), (), s32[]{:S(2)}) async-start(), calls=%async_computation.3 | async-start | bytes 524288 | tf_op jit(solution)/shard_map/while/body/eval_jaxpr/psum | solution.py:20
  1389.2 32.4 %reduce-scatter.2.cloned.1.call-start = ((), (), s32[]{:S(2)}) async-start(), calls=%async_computation.2 | async-start | bytes 2621440 | tf_op jit(solution)/shard_map/reduce_scatter | solution.py:164
  (37 other events, 1692.2 us)
Sparse Core Ops, SparseCore 0:
  9.8 36.9 all-gather.1
  753.7 272.5 all-reduce.1
  1032.5 174.7 all-reduce.1
  1213.1 174.7 all-reduce.1
  1392.3 29.2 reduce-scatter.1
where the time goes:
time: 1430 us
  waiting for transfers between devices  576 us (40%)
  blocking collectives  419 us (29%)
  starting transfers between devices  264 us (18%)
  other arithmetic  105 us (7%)
  matrix products  25.5 us (2%)
  local copies, waits for them, and re-layouts  21.7 us (2%)
  between operations  15.9 us (1%)
    psum x3, blocking collectives, broadcast(): return lax.psum(block, axis)  410 us
    ppermute x48, waiting for transfers between devices, from_behind(): return lax.ppermute(array, axis, pairs)  302 us
    ppermute x48, starting transfers between devices, from_behind(): return lax.ppermute(array, axis, pairs)  264 us
    psum x3, waiting for transfers between devices, broadcast(): return lax.psum(block, axis)  220 us
    add x47, other arithmetic, relay(): return (received, decay_total[:, :, None] * received + local_state)  51.8 us
    reduce_scatter x1, waiting for transfers between devices, body(): lax.psum_scatter(jnp.dot(gated, w_out, preferred_element_type=jnp.float32...  31.2 us
  transfers between devices with their start and end apart: 53, of which 52 were waited for; matrix products, arithmetic and copies ran while one was open for 1% of the time, Pallas kernels for 0%

commit v1 on v0

--- a/solution.py
+++ b/solution.py
@@ -17,7 +17,8 @@
 
 def broadcast(block, axis, source):
     block = jnp.where(lax.axis_index(axis) == source, block, jnp.zeros_like(block))
-    return lax.psum(block, axis)
+    _pack_run = lambda my_data, link_axis: jnp.sum(lax.all_gather(my_data, link_axis), axis=0)
+    return _pack_run(block, axis)
 
 
 def block_pass(carry, pieces):

time: 1430 us -> 1220 us (0.85)
  blocking collectives: 419 us -> 253 us
  waiting for transfers between devices: 576 us -> 505 us
  other arithmetic: 105 us -> 135 us
    psum x3 -> x0, blocking collectives: 410 us -> none  [broadcast(): return lax.psum(block, axis)]
    all_gather x0 -> x3, blocking collectives: none -> 243 us  [broadcast(): lax.all_gather(my_data, link_axis)]
    psum x3 -> x0, waiting for transfers between devices: 220 us -> none  [broadcast(): return lax.psum(block, axis)]
    all_gather x0 -> x3, waiting for transfers between devices: none -> 149 us  [broadcast(): lax.all_gather(my_data, link_axis)]
    reduce_sum x0 -> x6, other arithmetic: none -> 27.2 us  [broadcast(): jnp.sum(lax.all_gather(my_data, link_axis), axis=0)]
where the time goes in v1:
time: 1220 us
  waiting for transfers between devices  505 us (41%)
  starting transfers between devices  264 us (22%)
  blocking collectives  253 us (21%)
  other arithmetic  135 us (11%)
  matrix products  25.5 us (2%)
  local copies, waits for them, and re-layouts  21.7 us (2%)
  between operations  15.8 us (1%)
    ppermute x48, waiting for transfers between devices, from_behind(): return lax.ppermute(array, axis, pairs)  302 us
    ppermute x48, starting transfers between devices, from_behind(): return lax.ppermute(array, axis, pairs)  263 us
    all_gather x3, blocking collectives, broadcast(): lax.all_gather(my_data, link_axis)  243 us
    all_gather x3, waiting for transfers between devices, broadcast(): lax.all_gather(my_data, link_axis)  149 us
    add x47, other arithmetic, relay(): return (received, decay_total[:, :, None] * received + local_state)  51.8 us
    reduce_scatter x1, waiting for transfers between devices, body(): lax.psum_scatter(jnp.dot(gated, w_out, preferred_element_type=jnp.float32...  30.6 us
    reduce_sum x6, other arithmetic, broadcast(): jnp.sum(lax.all_gather(my_data, link_axis), axis=0)  27.2 us
  transfers between devices with their start and end apart: 53, of which 52 were waited for; matrix products, arithmetic and copies ran while one was open for 1% of the time, Pallas kernels for 0%

profile of v1, /device:TPU:1, one launch (start us, length us, event | category | flops | bytes accessed | tf_op | source)
XLA Modules:
  0.0 1221.6 jit_solution(18345712619564535556)
XLA Ops:
  14.5 9.3 psum.7
  24.5 22.2 %all-gather.3.cloned.1.call-done = bf16[512,2048]{1,0:T(8,128)(2,1)} async-done(((bf16[512,512]{1,0:T(8,128)(2,1)}), bf16[512,2048]{1,0:T(8,128)(2,1)}) %all-gather.3.cloned.1.call-update) | async-done | bytes 2097168 | tf_op jit(solution)/shard_map/all_gather | solution.py:87
  64.2 61.5 %while.53 = (s32[]{:T(128)}, f32[1,256,512]{2,1,0:T(8,128)S(1)}, f32[1,256]{1,0:T(1,128)S(1)}, f32[8,64,1,512]{3,1,2,0:T(8,128)}, f32[8,1,256,512]{3,2,1,0:T(8,1...) while((s32[]{:T(128)}, f32[1,256,512]{2,1,0:T(8,128)S(1)}, ...), condition=%wide.region_9.10_spmd.clone, body=%wide.region_7.9_spmd.clone.sunk | while | flops 27890436 | bytes 12177578 | solution.py:127
  126.5 613.5 %while.52 = (s32[]{:T(128)}, f32[1,256,512]{2,1,0:T(8,128)}, f32[1,256,512]{2,1,0:T(8,128)}, pred[]{:T(512)}, f32[1,256]{1,0:T(1,128)S(1)}, /*index=5*/f32[1,256,512]{2,1,0:T(8,128)S(1)}, s32[]{:T(128)}) while((s32[]{:T(128)}, f32[1,256,512]{2,1,0:T(8,128)}, f32[1,256,512]{2,1,0:T(8,128)}, pred[]{:T(512)}, f32[1,256]{1,0:T(1,128)S(1)}, ...), condition=%wide.region_11.12_spmd, body=%wide.region_10.11_spmd.sunk | while | flops 393218 | bytes 4195446 | solution.py:146
  140.2 6.4 collective-permute-done
  152.0 6.4 collective-permute-done
  163.8 6.4 collective-permute-done
  175.6 6.4 collective-permute-done
  199.2 6.4 collective-permute-done
  222.8 6.4 collective-permute-done
  234.6 6.4 collective-permute-done
  258.2 6.4 collective-permute-done
  281.9 6.4 collective-permute-done
  293.7 6.4 collective-permute-done
  305.5 6.4 collective-permute-done
  317.3 6.4 collective-permute-done
  356.8 6.4 collective-permute-done
  370.7 6.4 collective-permute-done
  398.6 6.4 collective-permute-done
  412.5 6.4 collective-permute-done
  426.4 6.4 collective-permute-done
  748.9 432.4 %while.54 = (s32[]{:T(128)}, f32[2,1,256,512]{3,2,1,0:T(8,128)}, bf16[2,3,1,1024]{3,2,1,0:T(2,128)(2,1)S(1)}, s32[2]{0:T(128)S(1)}, s32[3]{0:T(128)S(1)}, /*inde...) while((s32[]{:T(128)}, f32[2,1,256,512]{3,2,1,0:T(8,128)}, ...), condition=%wide.region_18.19_spmd.clone, body=%wide.region_14.18_spmd.clone.sunk | while | flops 9252884 | bytes 72931576 | solution.py:193
  751.0 146.1 %all_gather.37 = bf16[64,3,1,1024]{3,1,2,0:T(4,128)(2,1)S(1)} all-gather(bf16[1,3,1,1024]{3,1,2,0:T(4,128)(2,1)S(1)} %broadcast_select_fusion.12), channel_id=1, replica_groups=mesh['seq'=64,'tensor'=4] {'seq'}, dimensions={0}, use_global_device_ids=true | all-gather | bytes 399360 | tf_op jit(solution)/shard_map/while/body/eval_jaxpr/all_gather | solution.py:20
  897.4 50.5 %all-gather.5.cloned.1.call-done = bf16[64,1,256,512]{3,2,1,0:T(8,128)(2,1)} async-done(((bf16[1,1,256,512]{3,2,1,0:T(8,128)(2,1)}), bf16[64,1,256,512]{3,2,1,0:T(8,128)(2,1)}) %all-gather.5.cloned.1.call-update) | async-done | bytes 16777232 | tf_op jit(solution)/shard_map/while/body/eval_jaxpr/all_gather | solution.py:20
  947.8 8.8 reduce_sum.119
  960.0 48.6 %all_gather.37 = bf16[64,3,1,1024]{3,1,2,0:T(4,128)(2,1)S(1)} all-gather(bf16[1,3,1,1024]{3,1,2,0:T(4,128)(2,1)S(1)} %broadcast_select_fusion.12), channel_id=1, replica_groups=mesh['seq'=64,'tensor'=4] {'seq'}, dimensions={0}, use_global_device_ids=true | all-gather | bytes 399360 | tf_op jit(solution)/shard_map/while/body/eval_jaxpr/all_gather | solution.py:20
  1009.0 49.4 %all-gather.5.cloned.1.call-done = bf16[64,1,256,512]{3,2,1,0:T(8,128)(2,1)} async-done(((bf16[1,1,256,512]{3,2,1,0:T(8,128)(2,1)}), bf16[64,1,256,512]{3,2,1,0:T(8,128)(2,1)}) %all-gather.5.cloned.1.call-update) | async-done | bytes 16777232 | tf_op jit(solution)/shard_map/while/body/eval_jaxpr/all_gather | solution.py:20
  1058.4 8.8 reduce_sum.119
  1071.8 48.6 %all_gather.37 = bf16[64,3,1,1024]{3,1,2,0:T(4,128)(2,1)S(1)} all-gather(bf16[1,3,1,1024]{3,1,2,0:T(4,128)(2,1)S(1)} %broadcast_select_fusion.12), channel_id=1, replica_groups=mesh['seq'=64,'tensor'=4] {'seq'}, dimensions={0}, use_global_device_ids=true | all-gather | bytes 399360 | tf_op jit(solution)/shard_map/while/body/eval_jaxpr/all_gather | solution.py:20
  1120.8 49.1 %all-gather.5.cloned.1.call-done = bf16[64,1,256,512]{3,2,1,0:T(8,128)(2,1)} async-done(((bf16[1,1,256,512]{3,2,1,0:T(8,128)(2,1)}), bf16[64,1,256,512]{3,2,1,0:T(8,128)(2,1)}) %all-gather.5.cloned.1.call-update) | async-done | bytes 16777232 | tf_op jit(solution)/shard_map/while/body/eval_jaxpr/all_gather | solution.py:20
  1169.9 8.8 reduce_sum.119
  1182.5 30.6 %reduce-scatter.2.cloned.1.call-done = bf16[128,2048]{1,0:T(8,128)(2,1)} async-done(((bf16[512,2048]{1,0:T(8,128)(2,1)}), bf16[128,2048]{1,0:T(8,128)(2,1)}) %reduce-scatter.2.cloned.1.call-update) | async-done | bytes 524304 | tf_op jit(solution)/shard_map/reduce_scatter | solution.py:165
  (370 shorter events, 612.8 us)
Async XLA Ops:
  7.2 39.6 %all-gather.3.cloned.1.call-start = ((), (), s32[]{:S(2)}) async-start(), calls=%async_computation.1 | async-start | bytes 2621440 | tf_op jit(solution)/shard_map/all_gather | solution.py:87
  350.4 12.8 %collective-permute-start = (f32[1,256,512]{2,1,0:T(8,128)}, f32[1,256,512]{2,1,0:T(8,128)S(1)}, u32[]{:S(2)}, u32[]{:S(2)}) collective-permute-start(f32[1,256,512]{2,1,0:T(8,128)} %get-tuple-element.692), channel_id=1, source_target_pairs={{0,4},{4,8},{8,12},{12,16},{16,20},{20,24},{24,28},{28,32},{32,36}... | collective-permute-start | bytes 1572872 | tf_op jit(solution)/shard_map/while/body/eval_jaxpr/ppermute | solution.py:15
  364.4 12.8 %collective-permute-start = (f32[1,256,512]{2,1,0:T(8,128)}, f32[1,256,512]{2,1,0:T(8,128)S(1)}, u32[]{:S(2)}, u32[]{:S(2)}) collective-permute-start(f32[1,256,512]{2,1,0:T(8,128)} %get-tuple-element.692), channel_id=1, source_target_pairs={{0,4},{4,8},{8,12},{12,16},{16,20},{20,24},{24,28},{28,32},{32,36}... | collective-permute-start | bytes 1572872 | tf_op jit(solution)/shard_map/while/body/eval_jaxpr/ppermute | solution.py:15
  378.3 12.8 %collective-permute-start = (f32[1,256,512]{2,1,0:T(8,128)}, f32[1,256,512]{2,1,0:T(8,128)S(1)}, u32[]{:S(2)}, u32[]{:S(2)}) collective-permute-start(f32[1,256,512]{2,1,0:T(8,128)} %get-tuple-element.692), channel_id=1, source_target_pairs={{0,4},{4,8},{8,12},{12,16},{16,20},{20,24},{24,28},{28,32},{32,36}... | collective-permute-start | bytes 1572872 | tf_op jit(solution)/shard_map/while/body/eval_jaxpr/ppermute | solution.py:15
  392.2 12.8 %collective-permute-start = (f32[1,256,512]{2,1,0:T(8,128)}, f32[1,256,512]{2,1,0:T(8,128)S(1)}, u32[]{:S(2)}, u32[]{:S(2)}) collective-permute-start(f32[1,256,512]{2,1,0:T(8,128)} %get-tuple-element.692), channel_id=1, source_target_pairs={{0,4},{4,8},{8,12},{12,16},{16,20},{20,24},{24,28},{28,32},{32,36}... | collective-permute-start | bytes 1572872 | tf_op jit(solution)/shard_map/while/body/eval_jaxpr/ppermute | solution.py:15
  406.1 12.8 %collective-permute-start = (f32[1,256,512]{2,1,0:T(8,128)}, f32[1,256,512]{2,1,0:T(8,128)S(1)}, u32[]{:S(2)}, u32[]{:S(2)}) collective-permute-start(f32[1,256,512]{2,1,0:T(8,128)} %get-tuple-element.692), channel_id=1, source_target_pairs={{0,4},{4,8},{8,12},{12,16},{16,20},{20,24},{24,28},{28,32},{32,36}... | collective-permute-start | bytes 1572872 | tf_op jit(solution)/shard_map/while/body/eval_jaxpr/ppermute | solution.py:15
  420.0 12.8 %collective-permute-start = (f32[1,256,512]{2,1,0:T(8,128)}, f32[1,256,512]{2,1,0:T(8,128)S(1)}, u32[]{:S(2)}, u32[]{:S(2)}) collective-permute-start(f32[1,256,512]{2,1,0:T(8,128)} %get-tuple-element.692), channel_id=1, source_target_pairs={{0,4},{4,8},{8,12},{12,16},{16,20},{20,24},{24,28},{28,32},{32,36}... | collective-permute-start | bytes 1572872 | tf_op jit(solution)/shard_map/while/body/eval_jaxpr/ppermute | solution.py:15
  433.9 12.8 %collective-permute-start = (f32[1,256,512]{2,1,0:T(8,128)}, f32[1,256,512]{2,1,0:T(8,128)S(1)}, u32[]{:S(2)}, u32[]{:S(2)}) collective-permute-start(f32[1,256,512]{2,1,0:T(8,128)} %get-tuple-element.692), channel_id=1, source_target_pairs={{0,4},{4,8},{8,12},{12,16},{16,20},{20,24},{24,28},{28,32},{32,36}... | collective-permute-start | bytes 1572872 | tf_op jit(solution)/shard_map/while/body/eval_jaxpr/ppermute | solution.py:15
  447.8 12.8 %collective-permute-start = (f32[1,256,512]{2,1,0:T(8,128)}, f32[1,256,512]{2,1,0:T(8,128)S(1)}, u32[]{:S(2)}, u32[]{:S(2)}) collective-permute-start(f32[1,256,512]{2,1,0:T(8,128)} %get-tuple-element.692), channel_id=1, source_target_pairs={{0,4},{4,8},{8,12},{12,16},{16,20},{20,24},{24,28},{28,32},{32,36}... | collective-permute-start | bytes 1572872 | tf_op jit(solution)/shard_map/while/body/eval_jaxpr/ppermute | solution.py:15
  461.7 12.8 %collective-permute-start = (f32[1,256,512]{2,1,0:T(8,128)}, f32[1,256,512]{2,1,0:T(8,128)S(1)}, u32[]{:S(2)}, u32[]{:S(2)}) collective-permute-start(f32[1,256,512]{2,1,0:T(8,128)} %get-tuple-element.692), channel_id=1, source_target_pairs={{0,4},{4,8},{8,12},{12,16},{16,20},{20,24},{24,28},{28,32},{32,36}... | collective-permute-start | bytes 1572872 | tf_op jit(solution)/shard_map/while/body/eval_jaxpr/ppermute | solution.py:15
  475.6 12.8 %collective-permute-start = (f32[1,256,512]{2,1,0:T(8,128)}, f32[1,256,512]{2,1,0:T(8,128)S(1)}, u32[]{:S(2)}, u32[]{:S(2)}) collective-permute-start(f32[1,256,512]{2,1,0:T(8,128)} %get-tuple-element.692), channel_id=1, source_target_pairs={{0,4},{4,8},{8,12},{12,16},{16,20},{20,24},{24,28},{28,32},{32,36}... | collective-permute-start | bytes 1572872 | tf_op jit(solution)/shard_map/while/body/eval_jaxpr/ppermute | solution.py:15
  489.6 12.8 %collective-permute-start = (f32[1,256,512]{2,1,0:T(8,128)}, f32[1,256,512]{2,1,0:T(8,128)S(1)}, u32[]{:S(2)}, u32[]{:S(2)}) collective-permute-start(f32[1,256,512]{2,1,0:T(8,128)} %get-tuple-element.692), channel_id=1, source_target_pairs={{0,4},{4,8},{8,12},{12,16},{16,20},{20,24},{24,28},{28,32},{32,36}... | collective-permute-start | bytes 1572872 | tf_op jit(solution)/shard_map/while/body/eval_jaxpr/ppermute | solution.py:15
  503.5 12.8 %collective-permute-start = (f32[1,256,512]{2,1,0:T(8,128)}, f32[1,256,512]{2,1,0:T(8,128)S(1)}, u32[]{:S(2)}, u32[]{:S(2)}) collective-permute-start(f32[1,256,512]{2,1,0:T(8,128)} %get-tuple-element.692), channel_id=1, source_target_pairs={{0,4},{4,8},{8,12},{12,16},{16,20},{20,24},{24,28},{28,32},{32,36}... | collective-permute-start | bytes 1572872 | tf_op jit(solution)/shard_map/while/body/eval_jaxpr/ppermute | solution.py:15
  517.4 12.8 %collective-permute-start = (f32[1,256,512]{2,1,0:T(8,128)}, f32[1,256,512]{2,1,0:T(8,128)S(1)}, u32[]{:S(2)}, u32[]{:S(2)}) collective-permute-start(f32[1,256,512]{2,1,0:T(8,128)} %get-tuple-element.692), channel_id=1, source_target_pairs={{0,4},{4,8},{8,12},{12,16},{16,20},{20,24},{24,28},{28,32},{32,36}... | collective-permute-start | bytes 1572872 | tf_op jit(solution)/shard_map/while/body/eval_jaxpr/ppermute | solution.py:15
  531.3 12.8 %collective-permute-start = (f32[1,256,512]{2,1,0:T(8,128)}, f32[1,256,512]{2,1,0:T(8,128)S(1)}, u32[]{:S(2)}, u32[]{:S(2)}) collective-permute-start(f32[1,256,512]{2,1,0:T(8,128)} %get-tuple-element.692), channel_id=1, source_target_pairs={{0,4},{4,8},{8,12},{12,16},{16,20},{20,24},{24,28},{28,32},{32,36}... | collective-permute-start | bytes 1572872 | tf_op jit(solution)/shard_map/while/body/eval_jaxpr/ppermute | solution.py:15
  545.2 12.8 %collective-permute-start = (f32[1,256,512]{2,1,0:T(8,128)}, f32[1,256,512]{2,1,0:T(8,128)S(1)}, u32[]{:S(2)}, u32[]{:S(2)}) collective-permute-start(f32[1,256,512]{2,1,0:T(8,128)} %get-tuple-element.692), channel_id=1, source_target_pairs={{0,4},{4,8},{8,12},{12,16},{16,20},{20,24},{24,28},{28,32},{32,36}... | collective-permute-start | bytes 1572872 | tf_op jit(solution)/shard_map/while/body/eval_jaxpr/ppermute | solution.py:15
  559.1 12.8 %collective-permute-start = (f32[1,256,512]{2,1,0:T(8,128)}, f32[1,256,512]{2,1,0:T(8,128)S(1)}, u32[]{:S(2)}, u32[]{:S(2)}) collective-permute-start(f32[1,256,512]{2,1,0:T(8,128)} %get-tuple-element.692), channel_id=1, source_target_pairs={{0,4},{4,8},{8,12},{12,16},{16,20},{20,24},{24,28},{28,32},{32,36}... | collective-permute-start | bytes 1572872 | tf_op jit(solution)/shard_map/while/body/eval_jaxpr/ppermute | solution.py:15
  573.0 12.8 %collective-permute-start = (f32[1,256,512]{2,1,0:T(8,128)}, f32[1,256,512]{2,1,0:T(8,128)S(1)}, u32[]{:S(2)}, u32[]{:S(2)}) collective-permute-start(f32[1,256,512]{2,1,0:T(8,128)} %get-tuple-element.692), channel_id=1, source_target_pairs={{0,4},{4,8},{8,12},{12,16},{16,20},{20,24},{24,28},{28,32},{32,36}... | collective-permute-start | bytes 1572872 | tf_op jit(solution)/shard_map/while/body/eval_jaxpr/ppermute | solution.py:15
  586.9 12.8 %collective-permute-start = (f32[1,256,512]{2,1,0:T(8,128)}, f32[1,256,512]{2,1,0:T(8,128)S(1)}, u32[]{:S(2)}, u32[]{:S(2)}) collective-permute-start(f32[1,256,512]{2,1,0:T(8,128)} %get-tuple-element.692), channel_id=1, source_target_pairs={{0,4},{4,8},{8,12},{12,16},{16,20},{20,24},{24,28},{28,32},{32,36}... | collective-permute-start | bytes 1572872 | tf_op jit(solution)/shard_map/while/body/eval_jaxpr/ppermute | solution.py:15
  600.9 12.8 %collective-permute-start = (f32[1,256,512]{2,1,0:T(8,128)}, f32[1,256,512]{2,1,0:T(8,128)S(1)}, u32[]{:S(2)}, u32[]{:S(2)}) collective-permute-start(f32[1,256,512]{2,1,0:T(8,128)} %get-tuple-element.692), channel_id=1, source_target_pairs={{0,4},{4,8},{8,12},{12,16},{16,20},{20,24},{24,28},{28,32},{32,36}... | collective-permute-start | bytes 1572872 | tf_op jit(solution)/shard_map/while/body/eval_jaxpr/ppermute | solution.py:15
  614.8 12.8 %collective-permute-start = (f32[1,256,512]{2,1,0:T(8,128)}, f32[1,256,512]{2,1,0:T(8,128)S(1)}, u32[]{:S(2)}, u32[]{:S(2)}) collective-permute-start(f32[1,256,512]{2,1,0:T(8,128)} %get-tuple-element.692), channel_id=1, source_target_pairs={{0,4},{4,8},{8,12},{12,16},{16,20},{20,24},{24,28},{28,32},{32,36}... | collective-permute-start | bytes 1572872 | tf_op jit(solution)/shard_map/while/body/eval_jaxpr/ppermute | solution.py:15
  628.7 12.8 %collective-permute-start = (f32[1,256,512]{2,1,0:T(8,128)}, f32[1,256,512]{2,1,0:T(8,128)S(1)}, u32[]{:S(2)}, u32[]{:S(2)}) collective-permute-start(f32[1,256,512]{2,1,0:T(8,128)} %get-tuple-element.692), channel_id=1, source_target_pairs={{0,4},{4,8},{8,12},{12,16},{16,20},{20,24},{24,28},{28,32},{32,36}... | collective-permute-start | bytes 1572872 | tf_op jit(solution)/shard_map/while/body/eval_jaxpr/ppermute | solution.py:15
  642.6 12.8 %collective-permute-start = (f32[1,256,512]{2,1,0:T(8,128)}, f32[1,256,512]{2,1,0:T(8,128)S(1)}, u32[]{:S(2)}, u32[]{:S(2)}) collective-permute-start(f32[1,256,512]{2,1,0:T(8,128)} %get-tuple-element.692), channel_id=1, source_target_pairs={{0,4},{4,8},{8,12},{12,16},{16,20},{20,24},{24,28},{28,32},{32,36}... | collective-permute-start | bytes 1572872 | tf_op jit(solution)/shard_map/while/body/eval_jaxpr/ppermute | solution.py:15
  656.5 12.8 %collective-permute-start = (f32[1,256,512]{2,1,0:T(8,128)}, f32[1,256,512]{2,1,0:T(8,128)S(1)}, u32[]{:S(2)}, u32[]{:S(2)}) collective-permute-start(f32[1,256,512]{2,1,0:T(8,128)} %get-tuple-element.692), channel_id=1, source_target_pairs={{0,4},{4,8},{8,12},{12,16},{16,20},{20,24},{24,28},{28,32},{32,36}... | collective-permute-start | bytes 1572872 | tf_op jit(solution)/shard_map/while/body/eval_jaxpr/ppermute | solution.py:15
  670.4 12.8 %collective-permute-start = (f32[1,256,512]{2,1,0:T(8,128)}, f32[1,256,512]{2,1,0:T(8,128)S(1)}, u32[]{:S(2)}, u32[]{:S(2)}) collective-permute-start(f32[1,256,512]{2,1,0:T(8,128)} %get-tuple-element.692), channel_id=1, source_target_pairs={{0,4},{4,8},{8,12},{12,16},{16,20},{20,24},{24,28},{28,32},{32,36}... | collective-permute-start | bytes 1572872 | tf_op jit(solution)/shard_map/while/body/eval_jaxpr/ppermute | solution.py:15
  684.3 12.8 %collective-permute-start = (f32[1,256,512]{2,1,0:T(8,128)}, f32[1,256,512]{2,1,0:T(8,128)S(1)}, u32[]{:S(2)}, u32[]{:S(2)}) collective-permute-start(f32[1,256,512]{2,1,0:T(8,128)} %get-tuple-element.692), channel_id=1, source_target_pairs={{0,4},{4,8},{8,12},{12,16},{16,20},{20,24},{24,28},{28,32},{32,36}... | collective-permute-start | bytes 1572872 | tf_op jit(solution)/shard_map/while/body/eval_jaxpr/ppermute | solution.py:15
  712.2 12.8 %collective-permute-start = (f32[1,256,512]{2,1,0:T(8,128)}, f32[1,256,512]{2,1,0:T(8,128)S(1)}, u32[]{:S(2)}, u32[]{:S(2)}) collective-permute-start(f32[1,256,512]{2,1,0:T(8,128)} %get-tuple-element.692), channel_id=1, source_target_pairs={{0,4},{4,8},{8,12},{12,16},{16,20},{20,24},{24,28},{28,32},{32,36}... | collective-permute-start | bytes 1572872 | tf_op jit(solution)/shard_map/while/body/eval_jaxpr/ppermute | solution.py:15
  726.1 12.8 %collective-permute-start = (f32[1,256,512]{2,1,0:T(8,128)}, f32[1,256,512]{2,1,0:T(8,128)S(1)}, u32[]{:S(2)}, u32[]{:S(2)}) collective-permute-start(f32[1,256,512]{2,1,0:T(8,128)} %get-tuple-element.692), channel_id=1, source_target_pairs={{0,4},{4,8},{8,12},{12,16},{16,20},{20,24},{24,28},{28,32},{32,36}... | collective-permute-start | bytes 1572872 | tf_op jit(solution)/shard_map/while/body/eval_jaxpr/ppermute | solution.py:15
  748.9 198.9 %all-gather.5.cloned.1.call-start = ((), (), s32[]{:S(2)}) async-start(), calls=%async_computation.3 | async-start | bytes 17039360 | tf_op jit(solution)/shard_map/while/body/eval_jaxpr/all_gather | solution.py:20
  958.0 100.4 %all-gather.5.cloned.1.call-start = ((), (), s32[]{:S(2)}) async-start(), calls=%async_computation.3 | async-start | bytes 17039360 | tf_op jit(solution)/shard_map/while/body/eval_jaxpr/all_gather | solution.py:20
  1069.8 100.1 %all-gather.5.cloned.1.call-start = ((), (), s32[]{:S(2)}) async-start(), calls=%async_computation.3 | async-start | bytes 17039360 | tf_op jit(solution)/shard_map/while/body/eval_jaxpr/all_gather | solution.py:20
  1181.3 31.8 %reduce-scatter.2.cloned.1.call-start = ((), (), s32[]{:S(2)}) async-start(), calls=%async_computation.2 | async-start | bytes 2621440 | tf_op jit(solution)/shard_map/reduce_scatter | solution.py:165
  (34 other events, 1040.9 us)
Sparse Core Ops, SparseCore 0:
  9.8 36.9 all-gather.2
  753.0 194.7 all-gather.4
  962.1 96.2 all-gather.4
  1073.6 96.2 all-gather.4
  1184.3 28.7 reduce-scatter.1
